TPU v7x, 32 devices: a whole 2x2x4 slice. The times are simulated.
32 devices in a mesh: gx: 2 (over y), gy: 4 (over x, core), gz: 4 (over z).
Axes of the slice: x: 2, y: 2, z: 4, core: 2. Of those that a mesh axis runs over, the one named last changes fastest.
Arguments:
- density: float32 [16, 32, 512], P('gx', 'gy', 'gz'), may hold values from 0.5 to 2
- momentum: float32 [3, 16, 32, 512], P(None, 'gx', 'gy', 'gz'), may hold values from -3 to 3
- energy: float32 [16, 32, 512], P('gx', 'gy', 'gz'), may hold values from 1 to 4
- material: int32 [16, 32, 512], P('gx', 'gy', 'gz'), may hold values from 1 to 7
- tick_counts: int32 [3], replicated, may hold values from 1 to 4
Outputs:
- density_out: float32 [16, 32, 512], P('gx', 'gy', 'gz')
- momentum_out: float32 [3, 16, 32, 512], P(None, 'gx', 'gy', 'gz')
- energy_out: float32 [16, 32, 512], P('gx', 'gy', 'gz')
Inputs may be any that keep to these rules, and one draw needn't show every extreme that they name: `material`: bits 1, 2 and 4 say whether water, air and basalt are present in the cell; at least one is.
All inputs are finite; a program needn't handle non-finite values.
Results may differ from a plain program's by a relative error of at most 0.0003.
Values sent between devices are 32-bit elements; how exact they have to be, the bound alone decides.
A program may use at most 64 MiB of HBM per device.

v0:
```python
import functools

import jax
import jax.numpy as jnp
from jax import lax
from jax.experimental import pallas as pl
from jax.experimental.pallas import tpu as pltpu
from jax.sharding import PartitionSpec as P

MESH = pl.DeviceIdType.MESH
STEPS = 3
ITERS = 4
RHO_REF = (1.0, 0.5, 2.7)
BULK_LIN = (1.0, 0.0, 12.0)
BULK_QUAD = (6.0, 0.0, 12.0)
COEF_LOW = (0.7, 0.4, 0.5)
COEF_HIGH = (0.15, 0.0, 1.5)
ENERGY_REF = (3.0, 1.0, 20.0)
TIME_UNIT = 0.015
ROWS = 8
LANES = 128
AXES = ("gx", "gy", "gz")


def root(value):
    return value * lax.rsqrt(value)


def smooth_pos(value):
    return 0.5 * (value + root(value * value + 0.01))


def tillotson(phase, square, mass_heat, heat_scaled, k):
    gas = COEF_LOW[k]
    if COEF_HIGH[k] != 0.0:
        gas = gas + COEF_HIGH[k] * square / (heat_scaled[k] + square)
    total = gas * mass_heat
    if BULK_LIN[k] == 0.0 and BULK_QUAD[k] == 0.0:
        return total
    quad = BULK_QUAD[k] / RHO_REF[k]
    rest = BULK_LIN[k] - BULK_QUAD[k]
    if rest == 0.0:
        return total + phase * (quad / RHO_REF[k] * phase - quad)
    eta = phase if RHO_REF[k] == 1.0 else phase * (1.0 / RHO_REF[k])
    return total + (eta - 1.0) * (quad * phase + rest)


def shares_of(mask):
    high = mask >= 4.0
    rest = jnp.where(high, mask - 4.0, mask)
    middle = rest >= 2.0
    low = jnp.where(middle, rest - 2.0, rest)
    flags = [low, jnp.where(middle, 1.0, 0.0), jnp.where(high, 1.0, 0.0)]
    count = flags[0] + flags[1] + flags[2]
    part = 1.0 / count
    return [flag * part for flag in flags]


def state_eos(fields, shares):
    mixture = smooth_pos(fields[0])
    inverse = 1.0 / mixture
    velocity = [fields[1 + d] * inverse for d in range(3)]
    heat = smooth_pos(
        fields[4] * inverse
        - 0.5 * (velocity[0] * velocity[0] + velocity[1] * velocity[1] + velocity[2] * velocity[2])
    )
    amounts = [share * mixture for share in shares]
    squares = [
        BULK_LIN[k] / RHO_REF[k] + 0.1 + (COEF_LOW[k] + COEF_HIGH[k]) * heat for k in range(3)
    ]
    soft = [1.0 / square for square in squares]
    heat_scaled = [heat * (RHO_REF[k] * RHO_REF[k] / ENERGY_REF[k]) for k in range(3)]

    def all_pressures(phases):
        return [tillotson(r, r * r, r * heat, heat_scaled, k) for k, r in enumerate(phases)]

    phases = [mixture] * 3
    parts = [inverse] * 3
    weights = shares
    opened = None
    for _ in range(ITERS):
        pressures = all_pressures(phases)
        mean = weights[0] * pressures[0] + weights[1] * pressures[1] + weights[2] * pressures[2]
        gains = [parts[k] * soft[k] for k in range(3)]
        if opened is not None:
            mean = mean * opened
            gains = [gain * opened for gain in gains]
        phases = [
            phases[k] * (2.0 + jnp.tanh((mean - pressures[k]) * gains[k])) for k in range(3)
        ]
        parts = [1.0 / phase for phase in phases]
        weights = [amounts[k] * parts[k] for k in range(3)]
        closure = weights[0] + weights[1] + weights[2]
        phases = [phase * closure for phase in phases]
        opened = 1.0 / closure
    pressures = all_pressures(phases)
    pressure = opened * (weights[0] * pressures[0] + weights[1] * pressures[1] + weights[2] * pressures[2])
    sound = root(
        opened * (weights[0] * squares[0] + weights[1] * squares[1] + weights[2] * squares[2])
    )
    return pressure, [jnp.abs(velocity[d]) + sound for d in range(3)]


def minmod(left, right):
    return jnp.maximum(jnp.minimum(left, right), 0.0) + jnp.minimum(jnp.maximum(left, right), 0.0)


def side_flux(side, d):
    speed = side[1 + d] / smooth_pos(side[0])
    out = [side[0] * speed] + [side[1 + j] * speed for j in range(3)] + [(side[4] + side[5]) * speed]
    out[1 + d] = out[1 + d] + side[5]
    return out


def cell_sides(q, before, after, d):
    halves = [0.5 * minmod(q[f] - before[f], after[f] - q[f]) for f in range(6)]
    left = [q[f] + halves[f] for f in range(6)]
    right = [q[f] - halves[f] for f in range(6)]
    return left, side_flux(left, d), right, side_flux(right, d)


def join(left, flux_left, signal_left, right, flux_right, signal_right):
    wave = jnp.maximum(signal_left, signal_right)
    return [flux_left[f] + flux_right[f] - wave * (right[f] - left[f]) for f in range(5)]


def kernel(
    density, momentum, energy, material, ticks, final,
    state, side_y, pack_z, got_x, got_y, got_z,
    mask_raw, mask_own, mask_y, mask_got_x, mask_got_y,
    shares, shares_x, shares_y, own_p, own_s, div,
    send_sem, recv_sem, mask_send_sem, mask_recv_sem, load_sem,
):
    me = {axis: lax.axis_index(axis) for axis in AXES}
    size = {axis: lax.axis_size(axis) for axis in AXES}

    def peer(axis, way):
        n = size[axis]
        return {axis: lax.rem(me[axis] + (n - 1 if way == 0 else 1), n)}

    rows = state.shape[2]
    loads = [
        pltpu.make_async_copy(density, state.at[0, 0:1], load_sem.at[0]),
        pltpu.make_async_copy(momentum, state.at[0, 1:4], load_sem.at[1]),
        pltpu.make_async_copy(energy, state.at[0, 4:5], load_sem.at[2]),
        pltpu.make_async_copy(material, mask_raw, load_sem.at[3]),
    ]
    for load in loads:
        load.start()

    barrier = pltpu.get_barrier_semaphore()
    for axis in AXES:
        for way in range(2):
            pl.semaphore_signal(barrier, inc=1, device_id=peer(axis, way), device_id_type=MESH)

    for load in loads:
        load.wait()
    mask_own[...] = mask_raw[...].astype(jnp.float32)

    lane = lax.broadcasted_iota(jnp.int32, (ROWS, LANES), 1)
    octet = lax.div(lane, 8)
    spot = lax.rem(lane, 8)
    early = spot < 4
    lower_half = lane < LANES // 2
    at_edge = (lane < 2) | (lane >= LANES - 2)

    def gather_edges(read, count):
        packs = []
        for group in range(-(-count // 2)):
            total = None
            for f in range(group * 2, min(count, group * 2 + 2)):
                for x in range(ROWS):
                    start = 64 * (f % 2) + 8 * x
                    moved = pltpu.roll(read(f, x), (start + 4) % LANES, 1)
                    total = moved if total is None else jnp.where(octet == start // 8, moved, total)
            packs.append(total)
        return packs

    def tile(x):
        return pl.ds(x * ROWS, ROWS)

    def strided(y):
        return pl.ds(y, ROWS, stride=ROWS)

    for way in range(2):
        for k in range(2):
            mask_y[way, tile(k), :] = mask_own[strided(k if way == 0 else ROWS - 2 + k), :]

    def edge_rows(way):
        return pl.ds(0 if way == 0 else rows - 2 * ROWS, 2 * ROWS)

    def stage(step):
        for way in range(2):
            for f in range(5):
                for k in range(2):
                    side_y[step, way, f, tile(k), :] = state[
                        step, f, strided(k if way == 0 else ROWS - 2 + k), :
                    ]

    def rim_copy(step, a, way):
        if a == 0:
            src = state.at[step, :, edge_rows(way), :]
        elif a == 1:
            src = side_y.at[step, way]
        else:
            src = pack_z.at[step]
        return pltpu.make_async_remote_copy(
            src_ref=src,
            dst_ref=(got_x, got_y, got_z)[a].at[step, 1 - way],
            send_sem=send_sem.at[step, a, way],
            recv_sem=recv_sem.at[step, a, 1 - way],
            device_id=peer(AXES[a], way),
            device_id_type=MESH,
        )

    def mask_copy(a, way):
        return pltpu.make_async_remote_copy(
            src_ref=mask_own.at[edge_rows(way), :] if a == 0 else mask_y.at[way],
            dst_ref=(mask_got_x, mask_got_y)[a].at[1 - way],
            send_sem=mask_send_sem.at[a, way],
            recv_sem=mask_recv_sem.at[a, 1 - way],
            device_id=peer(AXES[a], way),
            device_id_type=MESH,
        )

    def arrive(step, a):
        for way in range(2):
            rim_copy(step, a, 1 - way).wait_recv()

    mask_pack = gather_edges(lambda f, x: mask_own[tile(x), :], 1)[0]
    for x in range(ROWS):
        for k, value in enumerate(shares_of(mask_own[tile(x), :])):
            shares[k, tile(x), :] = value

    def body(step, carry):
        @pl.when(step == 0)
        def _():
            pl.semaphore_wait(barrier, 6)

        packs = gather_edges(lambda f, x: state[step, f, tile(x), :], 5)
        packs[2] = jnp.where(lower_half, packs[2], pltpu.roll(mask_pack, 64, 1))
        for g in range(3):
            pack_z[step, g] = packs[g]
        for way in range(2):
            rim_copy(step, 2, way).start()
        for way in range(2):
            rim_copy(step, 0, way).start()
        stage(step)
        for way in range(2):
            rim_copy(step, 1, way).start()

        @pl.when(step == 0)
        def _():
            for a in (1, 0):
                for way in range(2):
                    mask_copy(a, way).start()

        chunk = 2 * ROWS
        for start in range(0, rows, chunk):
            at = pl.ds(start, chunk)
            p, signals = state_eos(
                [state[step, f, at, :] for f in range(5)], [shares[k, at, :] for k in range(3)]
            )
            own_p[at, :] = p
            for d in range(3):
                own_s[d, at, :] = signals[d]

        def own(a, i):
            at = tile(i) if a == 0 else strided(i)
            return [state[step, f, at, :] for f in range(5)] + [own_p[at, :]], own_s[a, at, :]

        def interior(a, emit):
            cells = {i: own(a, i) for i in range(ROWS)}
            sides = {
                i: cell_sides(cells[i][0], cells[i - 1][0], cells[i + 1][0], a) for i in range(1, ROWS - 1)
            }
            faces = {i: face(sides, cells, i) for i in range(1, ROWS - 2)}
            for i in range(2, ROWS - 2):
                emit(i, [faces[i][f] - faces[i - 1][f] for f in range(5)])
            return (
                {i: sides[i] for i in (1, ROWS - 2)},
                {i: faces[i] for i in (1, ROWS - 3)},
            )

        def face(sides, cells, i):
            left, flux_left, _, _ = sides[i]
            _, _, right, flux_right = sides[i + 1]
            return join(left, flux_left, cells[i][1], right, flux_right, cells[i + 1][1])

        def receive(a, way, mask_got, shares_got):
            rim_copy(step, a, 1 - way).wait_recv()

            @pl.when(step == 0)
            def _():
                mask_copy(a, 1 - way).wait_recv()
                for k, value in enumerate(shares_of(mask_got[way])):
                    shares_got[way, k] = value

        def border(a, way, got, shares_got, kept, emit):
            sides, faces = dict(kept[0]), dict(kept[1])
            near = (0, 1) if way == 0 else (ROWS - 2, ROWS - 1)
            cells = {i: own(a, i) for i in near}
            fields = [got[step, way, f] for f in range(5)]
            p, signals = state_eos(fields, [shares_got[way, k] for k in range(3)])
            for k in range(2):
                cells[k - 2 if way == 0 else ROWS + k] = (
                    [v[k * ROWS : (k + 1) * ROWS] for v in fields + [p]],
                    signals[a][k * ROWS : (k + 1) * ROWS],
                )
            for i in (-1, 0) if way == 0 else (ROWS - 1, ROWS):
                sides[i] = cell_sides(cells[i][0], cells[i - 1][0], cells[i + 1][0], a)
            for i in (-1, 0) if way == 0 else (ROWS - 2, ROWS - 1):
                faces[i] = face(sides, cells, i)
            for i in near:
                emit(i, [faces[i][f] - faces[i - 1][f] for f in range(5)])

        def emit_x(x, values):
            for f in range(5):
                div[0, f, tile(x), :] = values[f]

        def emit_y(y, values):
            for f in range(5):
                div[1, f, strided(y), :] = values[f]

        def up(v):
            return pltpu.roll(v, LANES - 1, 1)

        def down(v):
            return pltpu.roll(v, 1, 1)

        def depth(q, signal):
            left, flux_left, right, flux_right = cell_sides(q, [down(v) for v in q], [up(v) for v in q], 2)
            upper = join(
                left, flux_left, signal, [up(v) for v in right], [up(v) for v in flux_right], up(signal)
            )
            return [v - down(v) for v in upper]

        for x in range(ROWS):
            at = tile(x)
            values = depth([state[step, f, at, :] for f in range(5)] + [own_p[at, :]], own_s[2, at, :])
            for f in range(5):
                div[2, f, at, :] = values[f]
        edges = gather_edges(lambda f, x: own_p[tile(x), :] if f == 0 else own_s[2, tile(x), :], 2)[0]
        kept_y = interior(1, emit_y)
        kept_x = interior(0, emit_x)

        for way in (1, 0):
            receive(1, way, mask_got_y, shares_y)
        for way in (1, 0):
            border(1, way, got_y, shares_y, kept_y, emit_y)

        arrive(step, 2)
        for way in (1, 0):
            receive(0, way, mask_got_x, shares_x)
        rim_packs = [jnp.where(early, got_z[step, 0, g], got_z[step, 1, g]) for g in range(3)]

        def align(pack, f):
            return pack[f // 2] if f % 2 == 0 else pltpu.roll(pack[f // 2], LANES // 2, 1)

        rim = [align(rim_packs, f) for f in range(5)]
        p, signals = state_eos(rim, shares_of(jnp.where(lower_half, align(rim_packs, 5), 1.0)))
        outside = rim + [p, signals[2]]
        inside = [align([pack_z[step, g] for g in range(3)], f) for f in range(5)]
        inside += [edges, pltpu.roll(edges, LANES // 2, 1)]
        window = [
            jnp.where(
                lower_half,
                jnp.where(early, inside[f], outside[f]),
                pltpu.roll(jnp.where(early, outside[f], inside[f]), LANES // 2, 1),
            )
            for f in range(7)
        ]
        ends = [
            jnp.where(early, v, pltpu.roll(v, LANES // 2, 1)) for v in depth(window[:6], window[6])
        ]

        scale = ticks[step].astype(jnp.float32) * TIME_UNIT * 0.5

        def advance(x):
            at = tile(x)
            for f in range(5):
                end = pltpu.roll(ends[f], (LANES - 4 - 8 * x) % LANES, 1)
                total = div[0, f, at, :] + div[1, f, at, :] + jnp.where(at_edge, end, div[2, f, at, :])
                state[step + 1, f, at, :] = state[step, f, at, :] - scale * total

        for way in (1, 0):
            border(0, way, got_x, shares_x, kept_x, emit_x)
        for x in range(ROWS):
            advance(x)
        return carry

    lax.fori_loop(0, STEPS, body, 0)

    final[...] = state[STEPS]
    for way in range(2):
        for a in range(3):
            for step in range(STEPS):
                rim_copy(step, a, way).wait_send()
        for a in range(2):
            mask_copy(a, way).wait_send()


def store(final, density, momentum, energy, sem):
    stores = [
        pltpu.make_async_copy(final.at[0:1], density, sem.at[0]),
        pltpu.make_async_copy(final.at[1:4], momentum, sem.at[1]),
        pltpu.make_async_copy(final.at[4:5], energy, sem.at[2]),
    ]
    for copy in stores:
        copy.start()
    for copy in stores:
        copy.wait()


def solution(mesh):
    def per_device(density, momentum, energy, material, tick_counts):
        nx, ny, nz = density.shape
        assert (nx, ny, nz) == (ROWS, ROWS, LANES), "tile shape"
        rows = nx * ny
        f32 = jnp.float32
        vmem = pl.BlockSpec(memory_space=pltpu.VMEM)
        rim = (2 * ROWS, LANES)
        anywhere = pl.BlockSpec(memory_space=pl.ANY)
        final = pl.pallas_call(
            kernel,
            out_shape=pltpu.VMEM((5, rows, nz), f32),
            in_specs=[anywhere] * 4 + [pl.BlockSpec(memory_space=pltpu.SMEM)],
            out_specs=vmem,
            scratch_shapes=[
                pltpu.VMEM((STEPS + 1, 5, rows, nz), f32),
                pltpu.VMEM((STEPS, 2, 5) + rim, f32),
                pltpu.VMEM((STEPS, 3, ROWS, LANES), f32),
                pltpu.VMEM((STEPS, 2, 5) + rim, f32),
                pltpu.VMEM((STEPS, 2, 5) + rim, f32),
                pltpu.VMEM((STEPS, 2, 3, ROWS, LANES), f32),
                pltpu.VMEM((rows, nz), jnp.int32),
                pltpu.VMEM((rows, nz), f32),
                pltpu.VMEM((2,) + rim, f32),
                pltpu.VMEM((2,) + rim, f32),
                pltpu.VMEM((2,) + rim, f32),
                pltpu.VMEM((3, rows, nz), f32),
                pltpu.VMEM((2, 3) + rim, f32),
                pltpu.VMEM((2, 3) + rim, f32),
                pltpu.VMEM((rows, nz), f32),
                pltpu.VMEM((3, rows, nz), f32),
                pltpu.VMEM((3, 5, rows, nz), f32),
                pltpu.SemaphoreType.DMA((STEPS, 3, 2)),
                pltpu.SemaphoreType.DMA((STEPS, 3, 2)),
                pltpu.SemaphoreType.DMA((2, 2)),
                pltpu.SemaphoreType.DMA((2, 2)),
                pltpu.SemaphoreType.DMA((4,)),
            ],
            compiler_params=pltpu.CompilerParams(collective_id=0, has_side_effects=True),
            name="hydro_steps",
        )(
            density.reshape(1, rows, nz),
            momentum.reshape(3, rows, nz),
            energy.reshape(1, rows, nz),
            material.reshape(rows, nz),
            tick_counts,
        )
        outs = pl.pallas_call(
            store,
            out_shape=tuple(jax.ShapeDtypeStruct((n, rows, nz), f32) for n in (1, 3, 1)),
            in_specs=[anywhere],
            out_specs=(anywhere,) * 3,
            scratch_shapes=[pltpu.SemaphoreType.DMA((3,))],
            compiler_params=pltpu.CompilerParams(vmem_limit_bytes=1 << 20),
            name="store_state",
        )(final)
        return (
            outs[0].reshape(nx, ny, nz),
            outs[1].reshape(3, nx, ny, nz),
            outs[2].reshape(nx, ny, nz),
        )

    placed = P("gx", "gy", "gz")
    moved = P(None, "gx", "gy", "gz")
    return jax.shard_map(
        per_device,
        mesh=mesh,
        in_specs=(placed, moved, placed, placed, P()),
        out_specs=(placed, moved, placed),
        check_vma=False,
    )
```

profile of v0, /device:TPU:0, one launch (start us, length us, event | category | flops | bytes accessed | tf_op | source)
XLA Modules:
  0.0 21.7 jit_solution(8364927489908807880)
XLA Ops:
  0.6 20.4 %hydro_steps.1.final = f32[5,64,128]{2,1,0:T(8,128)S(1)} custom-call(f32[1,64,128]{2,1,0:T(8,128)} %bitcast.8, f32[3,64,128]{2,1,0:T(8,128)} %bitcast.7, f32[1,64,128]{2,1,0:T(8,128)} %bitcast.9, s32[64,128]{1,0:T(8,128)} %bitcast.10, s32[3]{0:T(128)} %ticks.1), custom_call_target="tpu_custom_call" | custom-call | tf_op jit(solution)/shard_map/hydro_steps/pallas_call | solution.py:424
  21.0 0.7 %store_state.1 = (f32[1,64,128]{2,1,0:T(8,128)}, f32[3,64,128]{2,1,0:T(8,128)}, f32[1,64,128]{2,1,0:T(8,128)}) custom-call(f32[5,64,128]{2,1,0:T(8,128)S(1)} %hydro_steps.1.final), custom_call_target="tpu_custom_call" | custom-call | tf_op jit(solution)/shard_map/store_state/pallas_call | solution.py:462
where the time goes:
time: 21.9 us; the launch traced here: 21.7 us
  Pallas kernels  21.1 us (96%)
  between operations  0.64 us (3%)
    pallas_call x1, Pallas kernels, per_device(): pl.pallas_call(kernel, out_shape=pltpu.VMEM((5, rows, nz), f32), in_specs...  20.4 us
    pallas_call x1, Pallas kernels, per_device(): pl.pallas_call(store, out_shape=tuple((jax.ShapeDtypeStruct((n, rows, nz)...  0.69 us

commit v1 on v0

--- a/solution.py
+++ b/solution.py
@@ -125,11 +125,10 @@
 
 
 def kernel(
-    density, momentum, energy, material, ticks, final,
+    density, momentum, energy, material, ticks_hbm, final,
     state, side_y, pack_z, got_x, got_y, got_z,
-    mask_raw, mask_own, mask_y, mask_got_x, mask_got_y,
-    shares, shares_x, shares_y, own_p, own_s, div,
-    send_sem, recv_sem, mask_send_sem, mask_recv_sem, load_sem,
+    mask_raw, ticks, shares, shares_x, shares_y, own_p, own_s, div,
+    send_sem, recv_sem, load_sem,
 ):
     me = {axis: lax.axis_index(axis) for axis in AXES}
     size = {axis: lax.axis_size(axis) for axis in AXES}
@@ -139,23 +138,23 @@
         return {axis: lax.rem(me[axis] + (n - 1 if way == 0 else 1), n)}
 
     rows = state.shape[2]
+    barrier = pltpu.get_barrier_semaphore()
+
+    def greet(axis):
+        for way in range(2):
+            pl.semaphore_signal(barrier, inc=1, device_id=peer(axis, way), device_id_type=MESH)
+
     loads = [
-        pltpu.make_async_copy(density, state.at[0, 0:1], load_sem.at[0]),
-        pltpu.make_async_copy(momentum, state.at[0, 1:4], load_sem.at[1]),
-        pltpu.make_async_copy(energy, state.at[0, 4:5], load_sem.at[2]),
-        pltpu.make_async_copy(material, mask_raw, load_sem.at[3]),
+        pltpu.make_async_copy(material, mask_raw, load_sem.at[0]),
+        pltpu.make_async_copy(density, state.at[0, 0:1], load_sem.at[1]),
+        pltpu.make_async_copy(momentum, state.at[0, 1:4], load_sem.at[2]),
+        pltpu.make_async_copy(energy, state.at[0, 4:5], load_sem.at[3]),
+        pltpu.make_async_copy(ticks_hbm, ticks, load_sem.at[4]),
     ]
     for load in loads:
         load.start()
-
-    barrier = pltpu.get_barrier_semaphore()
-    for axis in AXES:
-        for way in range(2):
-            pl.semaphore_signal(barrier, inc=1, device_id=peer(axis, way), device_id_type=MESH)
-
-    for load in loads:
-        load.wait()
-    mask_own[...] = mask_raw[...].astype(jnp.float32)
+    for axis in ("gz", "gx", "gy"):
+        greet(axis)
 
     lane = lax.broadcasted_iota(jnp.int32, (ROWS, LANES), 1)
     octet = lax.div(lane, 8)
@@ -182,79 +181,79 @@
     def strided(y):
         return pl.ds(y, ROWS, stride=ROWS)
 
-    for way in range(2):
-        for k in range(2):
-            mask_y[way, tile(k), :] = mask_own[strided(k if way == 0 else ROWS - 2 + k), :]
-
     def edge_rows(way):
         return pl.ds(0 if way == 0 else rows - 2 * ROWS, 2 * ROWS)
 
-    def stage(step):
-        for way in range(2):
-            for f in range(5):
-                for k in range(2):
-                    side_y[step, way, f, tile(k), :] = state[
-                        step, f, strided(k if way == 0 else ROWS - 2 + k), :
-                    ]
+    def sent(step):
+        return 6 if step == 0 else 5
 
     def rim_copy(step, a, way):
+        fields = pl.ds(0, sent(step))
         if a == 0:
-            src = state.at[step, :, edge_rows(way), :]
+            src = state.at[step, fields, edge_rows(way), :]
         elif a == 1:
-            src = side_y.at[step, way]
+            src = side_y.at[step, way, fields]
         else:
             src = pack_z.at[step]
+        into = (got_x, got_y, got_z)[a].at[step, 1 - way]
         return pltpu.make_async_remote_copy(
             src_ref=src,
-            dst_ref=(got_x, got_y, got_z)[a].at[step, 1 - way],
+            dst_ref=into if a == 2 else into.at[fields],
             send_sem=send_sem.at[step, a, way],
             recv_sem=recv_sem.at[step, a, 1 - way],
             device_id=peer(AXES[a], way),
             device_id_type=MESH,
         )
 
-    def mask_copy(a, way):
-        return pltpu.make_async_remote_copy(
-            src_ref=mask_own.at[edge_rows(way), :] if a == 0 else mask_y.at[way],
-            dst_ref=(mask_got_x, mask_got_y)[a].at[1 - way],
-            send_sem=mask_send_sem.at[a, way],
-            recv_sem=mask_recv_sem.at[a, 1 - way],
-            device_id=peer(AXES[a], way),
-            device_id_type=MESH,
-        )
-
-    def arrive(step, a):
+    def send(step, a):
         for way in range(2):
-            rim_copy(step, a, 1 - way).wait_recv()
-
-    mask_pack = gather_edges(lambda f, x: mask_own[tile(x), :], 1)[0]
-    for x in range(ROWS):
-        for k, value in enumerate(shares_of(mask_own[tile(x), :])):
-            shares[k, tile(x), :] = value
-
-    def body(step, carry):
-        @pl.when(step == 0)
-        def _():
-            pl.semaphore_wait(barrier, 6)
-
+            rim_copy(step, a, way).start()
+
+    def arrive(step, a, way):
+        rim_copy(step, a, 1 - way).wait_recv()
+
+    def stage(step):
+        for way in range(2):
+            for f in range(sent(step)):
+                for k in range(2):
+                    side_y[step, way, f, tile(k), :] = state[
+                        step, f, strided(k if way == 0 else ROWS - 2 + k), :
+                    ]
+
+    def pack(step):
         packs = gather_edges(lambda f, x: state[step, f, tile(x), :], 5)
         packs[2] = jnp.where(lower_half, packs[2], pltpu.roll(mask_pack, 64, 1))
         for g in range(3):
             pack_z[step, g] = packs[g]
-        for way in range(2):
-            rim_copy(step, 2, way).start()
-        for way in range(2):
-            rim_copy(step, 0, way).start()
-        stage(step)
-        for way in range(2):
-            rim_copy(step, 1, way).start()
-
-        @pl.when(step == 0)
-        def _():
-            for a in (1, 0):
-                for way in range(2):
-                    mask_copy(a, way).start()
-
+
+    for load in loads:
+        load.wait()
+    state[0, 5] = mask_raw[...].astype(jnp.float32)
+    mask_pack = gather_edges(lambda f, x: state[0, 5, tile(x), :], 1)[0]
+    pack(0)
+    stage(0)
+    pl.semaphore_wait(barrier, 6)
+    for a in (2, 0, 1):
+        send(0, a)
+
+    for x in range(ROWS):
+        for k, value in enumerate(shares_of(state[0, 5, tile(x), :])):
+            shares[k, tile(x), :] = value
+
+    def up(v):
+        return pltpu.roll(v, LANES - 1, 1)
+
+    def down(v):
+        return pltpu.roll(v, 1, 1)
+
+    def depth(q, signal):
+        left, flux_left, right, flux_right = cell_sides(q, [down(v) for v in q], [up(v) for v in q], 2)
+        upper = join(
+            left, flux_left, signal, [up(v) for v in right], [up(v) for v in flux_right], up(signal)
+        )
+        return [v - down(v) for v in upper]
+
+    def body(step):
         chunk = 2 * ROWS
         for start in range(0, rows, chunk):
             at = pl.ds(start, chunk)
@@ -268,6 +267,11 @@
         def own(a, i):
             at = tile(i) if a == 0 else strided(i)
             return [state[step, f, at, :] for f in range(5)] + [own_p[at, :]], own_s[a, at, :]
+
+        def face(sides, cells, i):
+            left, flux_left, _, _ = sides[i]
+            _, _, right, flux_right = sides[i + 1]
+            return join(left, flux_left, cells[i][1], right, flux_right, cells[i + 1][1])
 
         def interior(a, emit):
             cells = {i: own(a, i) for i in range(ROWS)}
@@ -282,18 +286,9 @@
                 {i: faces[i] for i in (1, ROWS - 3)},
             )
 
-        def face(sides, cells, i):
-            left, flux_left, _, _ = sides[i]
-            _, _, right, flux_right = sides[i + 1]
-            return join(left, flux_left, cells[i][1], right, flux_right, cells[i + 1][1])
-
-        def receive(a, way, mask_got, shares_got):
-            rim_copy(step, a, 1 - way).wait_recv()
-
-            @pl.when(step == 0)
-            def _():
-                mask_copy(a, 1 - way).wait_recv()
-                for k, value in enumerate(shares_of(mask_got[way])):
+        def open_shares(way, got, shares_got):
+            if step == 0:
+                for k, value in enumerate(shares_of(got[0, way, 5])):
                     shares_got[way, k] = value
 
         def border(a, way, got, shares_got, kept, emit):
@@ -322,19 +317,6 @@
             for f in range(5):
                 div[1, f, strided(y), :] = values[f]
 
-        def up(v):
-            return pltpu.roll(v, LANES - 1, 1)
-
-        def down(v):
-            return pltpu.roll(v, 1, 1)
-
-        def depth(q, signal):
-            left, flux_left, right, flux_right = cell_sides(q, [down(v) for v in q], [up(v) for v in q], 2)
-            upper = join(
-                left, flux_left, signal, [up(v) for v in right], [up(v) for v in flux_right], up(signal)
-            )
-            return [v - down(v) for v in upper]
-
         for x in range(ROWS):
             at = tile(x)
             values = depth([state[step, f, at, :] for f in range(5)] + [own_p[at, :]], own_s[2, at, :])
@@ -345,13 +327,26 @@
         kept_x = interior(0, emit_x)
 
         for way in (1, 0):
-            receive(1, way, mask_got_y, shares_y)
+            arrive(step, 1, way)
         for way in (1, 0):
+            open_shares(way, got_y, shares_y)
             border(1, way, got_y, shares_y, kept_y, emit_y)
-
-        arrive(step, 2)
+        scale = ticks[step].astype(jnp.float32) * TIME_UNIT * 0.5
+        for x in range(ROWS):
+            at = tile(x)
+            for f in range(5):
+                part = div[1, f, at, :] + jnp.where(at_edge, 0.0, div[2, f, at, :])
+                if 2 <= x < ROWS - 2:
+                    part = part + div[0, f, at, :]
+                div[2, f, at, :] = part
+
+        arrive(step, 0, 1)
+        open_shares(1, got_x, shares_x)
+        border(0, 1, got_x, shares_x, kept_x, emit_x)
+
         for way in (1, 0):
-            receive(0, way, mask_got_x, shares_x)
+            arrive(step, 2, way)
+        arrive(step, 0, 0)
         rim_packs = [jnp.where(early, got_z[step, 0, g], got_z[step, 1, g]) for g in range(3)]
 
         def align(pack, f):
@@ -373,31 +368,37 @@
         ends = [
             jnp.where(early, v, pltpu.roll(v, LANES // 2, 1)) for v in depth(window[:6], window[6])
         ]
-
-        scale = ticks[step].astype(jnp.float32) * TIME_UNIT * 0.5
-
-        def advance(x):
+        open_shares(0, got_x, shares_x)
+        border(0, 0, got_x, shares_x, kept_x, emit_x)
+
+        last = step + 1 == STEPS
+        for x in (0, 1, ROWS - 2, ROWS - 1, *range(2, ROWS - 2)):
             at = tile(x)
             for f in range(5):
                 end = pltpu.roll(ends[f], (LANES - 4 - 8 * x) % LANES, 1)
-                total = div[0, f, at, :] + div[1, f, at, :] + jnp.where(at_edge, end, div[2, f, at, :])
-                state[step + 1, f, at, :] = state[step, f, at, :] - scale * total
-
-        for way in (1, 0):
-            border(0, way, got_x, shares_x, kept_x, emit_x)
-        for x in range(ROWS):
-            advance(x)
-        return carry
-
-    lax.fori_loop(0, STEPS, body, 0)
-
-    final[...] = state[STEPS]
+                total = div[2, f, at, :] + jnp.where(at_edge, end, 0.0)
+                if not 2 <= x < ROWS - 2:
+                    total = total + div[0, f, at, :]
+                value = state[step, f, at, :] - scale * total
+                if last:
+                    final[f, at, :] = value
+                else:
+                    state[step + 1, f, at, :] = value
+            if x == ROWS - 1 and not last:
+                send(step + 1, 0)
+        if not last:
+            pack(step + 1)
+            send(step + 1, 2)
+            stage(step + 1)
+            send(step + 1, 1)
+
+    for step in range(STEPS):
+        body(step)
+
     for way in range(2):
         for a in range(3):
             for step in range(STEPS):
                 rim_copy(step, a, way).wait_send()
-        for a in range(2):
-            mask_copy(a, way).wait_send()
 
 
 def store(final, density, momentum, energy, sem):
@@ -424,20 +425,17 @@
         final = pl.pallas_call(
             kernel,
             out_shape=pltpu.VMEM((5, rows, nz), f32),
-            in_specs=[anywhere] * 4 + [pl.BlockSpec(memory_space=pltpu.SMEM)],
+            in_specs=[anywhere] * 5,
             out_specs=vmem,
             scratch_shapes=[
-                pltpu.VMEM((STEPS + 1, 5, rows, nz), f32),
-                pltpu.VMEM((STEPS, 2, 5) + rim, f32),
+                pltpu.VMEM((STEPS, 6, rows, nz), f32),
+                pltpu.VMEM((STEPS, 2, 6) + rim, f32),
                 pltpu.VMEM((STEPS, 3, ROWS, LANES), f32),
-                pltpu.VMEM((STEPS, 2, 5) + rim, f32),
-                pltpu.VMEM((STEPS, 2, 5) + rim, f32),
+                pltpu.VMEM((STEPS, 2, 6) + rim, f32),
+                pltpu.VMEM((STEPS, 2, 6) + rim, f32),
                 pltpu.VMEM((STEPS, 2, 3, ROWS, LANES), f32),
                 pltpu.VMEM((rows, nz), jnp.int32),
-                pltpu.VMEM((rows, nz), f32),
-                pltpu.VMEM((2,) + rim, f32),
-                pltpu.VMEM((2,) + rim, f32),
-                pltpu.VMEM((2,) + rim, f32),
+                pltpu.SMEM((STEPS,), jnp.int32),
                 pltpu.VMEM((3, rows, nz), f32),
                 pltpu.VMEM((2, 3) + rim, f32),
                 pltpu.VMEM((2, 3) + rim, f32),
@@ -446,9 +444,7 @@
                 pltpu.VMEM((3, 5, rows, nz), f32),
                 pltpu.SemaphoreType.DMA((STEPS, 3, 2)),
                 pltpu.SemaphoreType.DMA((STEPS, 3, 2)),
-                pltpu.SemaphoreType.DMA((2, 2)),
-                pltpu.SemaphoreType.DMA((2, 2)),
-                pltpu.SemaphoreType.DMA((4,)),
+                pltpu.SemaphoreType.DMA((5,)),
             ],
             compiler_params=pltpu.CompilerParams(collective_id=0, has_side_effects=True),
             name="hydro_steps",

time: 21.9 us -> 20.8 us (0.950)
  Pallas kernels: 21.1 us -> 20 us
    pallas_call x1, Pallas kernels: 20.4 us -> 19.3 us  [per_device(): pl.pallas_call(kernel, out_shape=pltpu.VMEM((5, rows, nz), f32), in_specs...]
where the time goes in v1:
time: 20.8 us; the launch traced here: 20.7 us
  Pallas kernels  20 us (96%)
  between operations  0.64 us (3%)
    pallas_call x1, Pallas kernels, per_device(): pl.pallas_call(kernel, out_shape=pltpu.VMEM((5, rows, nz), f32), in_specs...  19.3 us
    pallas_call x1, Pallas kernels, per_device(): pl.pallas_call(store, out_shape=tuple((jax.ShapeDtypeStruct((n, rows, nz)...  0.69 us

profile of v1, /device:TPU:0, one launch (start us, length us, event | category | flops | bytes accessed | tf_op | source)
XLA Modules:
  0.0 20.7 jit_solution(10407624959488663061)
XLA Ops:
  0.6 19.3 %hydro_steps.1.final = f32[5,64,128]{2,1,0:T(8,128)S(1)} custom-call(f32[1,64,128]{2,1,0:T(8,128)} %bitcast.8, f32[3,64,128]{2,1,0:T(8,128)} %bitcast.7, f32[1,64,128]{2,1,0:T(8,128)} %bitcast.9, s32[64,128]{1,0:T(8,128)} %bitcast.10, s32[3]{0:T(128)} %ticks_hbm.1), custom_call_target="tpu_custom_call" | custom-call | tf_op jit(solution)/shard_map/hydro_steps/pallas_call | solution.py:425
  20.0 0.7 %store_state.1 = (f32[1,64,128]{2,1,0:T(8,128)}, f32[3,64,128]{2,1,0:T(8,128)}, f32[1,64,128]{2,1,0:T(8,128)}) custom-call(f32[5,64,128]{2,1,0:T(8,128)S(1)} %hydro_steps.1.final), custom_call_target="tpu_custom_call" | custom-call | tf_op jit(solution)/shard_map/store_state/pallas_call | solution.py:458

commit v2 on v1

--- a/solution.py
+++ b/solution.py
@@ -127,7 +127,7 @@
 def kernel(
     density, momentum, energy, material, ticks_hbm, final,
     state, side_y, pack_z, got_x, got_y, got_z,
-    mask_raw, ticks, shares, shares_x, shares_y, own_p, own_s, div,
+    mask_raw, ticks, shares, shares_x, shares_y, shares_z, own_p, own_s, div,
     send_sem, recv_sem, load_sem,
 ):
     me = {axis: lax.axis_index(axis) for axis in AXES}
@@ -158,22 +158,19 @@
 
     lane = lax.broadcasted_iota(jnp.int32, (ROWS, LANES), 1)
     octet = lax.div(lane, 8)
-    spot = lax.rem(lane, 8)
-    early = spot < 4
-    lower_half = lane < LANES // 2
-    at_edge = (lane < 2) | (lane >= LANES - 2)
-
-    def gather_edges(read, count):
-        packs = []
-        for group in range(-(-count // 2)):
-            total = None
-            for f in range(group * 2, min(count, group * 2 + 2)):
-                for x in range(ROWS):
-                    start = 64 * (f % 2) + 8 * x
-                    moved = pltpu.roll(read(f, x), (start + 4) % LANES, 1)
-                    total = moved if total is None else jnp.where(octet == start // 8, moved, total)
-            packs.append(total)
-        return packs
+    half = LANES // 2
+    lower_half = lane < half
+    is_out = lax.div(lane, half) + lax.div(lax.rem(lane, 8), 4) == 1
+    at_low = lane < 2
+    at_edge = at_low | (lane >= LANES - 2)
+
+    def edge_pack(read):
+        total = None
+        for x in range(ROWS):
+            for start in (8 * x, half + 8 * x):
+                moved = pltpu.roll(read(x), start + 4, 1)
+                total = moved if total is None else jnp.where(octet == start // 8, moved, total)
+        return total
 
     def tile(x):
         return pl.ds(x * ROWS, ROWS)
@@ -194,11 +191,11 @@
         elif a == 1:
             src = side_y.at[step, way, fields]
         else:
-            src = pack_z.at[step]
+            src = pack_z.at[step, fields]
         into = (got_x, got_y, got_z)[a].at[step, 1 - way]
         return pltpu.make_async_remote_copy(
             src_ref=src,
-            dst_ref=into if a == 2 else into.at[fields],
+            dst_ref=into.at[fields],
             send_sem=send_sem.at[step, a, way],
             recv_sem=recv_sem.at[step, a, 1 - way],
             device_id=peer(AXES[a], way),
@@ -221,15 +218,12 @@
                     ]
 
     def pack(step):
-        packs = gather_edges(lambda f, x: state[step, f, tile(x), :], 5)
-        packs[2] = jnp.where(lower_half, packs[2], pltpu.roll(mask_pack, 64, 1))
-        for g in range(3):
-            pack_z[step, g] = packs[g]
+        for f in range(sent(step)):
+            pack_z[step, f] = edge_pack(lambda x: state[step, f, tile(x), :])
 
     for load in loads:
         load.wait()
     state[0, 5] = mask_raw[...].astype(jnp.float32)
-    mask_pack = gather_edges(lambda f, x: state[0, 5, tile(x), :], 1)[0]
     pack(0)
     stage(0)
     pl.semaphore_wait(barrier, 6)
@@ -252,6 +246,30 @@
             left, flux_left, signal, [up(v) for v in right], [up(v) for v in flux_right], up(signal)
         )
         return [v - down(v) for v in upper]
+
+    def rim_depth(q, signal):
+        below = [down(v) for v in q]
+        above = [up(v) for v in q]
+        step_down = [q[f] - below[f] for f in range(6)]
+        step_up = [above[f] - q[f] for f in range(6)]
+        far_down = [below[f] - pltpu.roll(q[f], 2, 1) for f in range(6)]
+        far_up = [pltpu.roll(q[f], LANES - 2, 1) - above[f] for f in range(6)]
+        halves = [0.5 * minmod(step_down[f], step_up[f]) for f in range(6)]
+        halves_below = [0.5 * minmod(far_down[f], step_down[f]) for f in range(6)]
+        halves_above = [0.5 * minmod(step_up[f], far_up[f]) for f in range(6)]
+
+        def face(left, signal_left, right, signal_right):
+            return join(left, side_flux(left, 2), signal_left, right, side_flux(right, 2), signal_right)
+
+        upper = face(
+            [q[f] + halves[f] for f in range(6)], signal,
+            [above[f] - halves_above[f] for f in range(6)], up(signal),
+        )
+        lower = face(
+            [below[f] + halves_below[f] for f in range(6)], down(signal),
+            [q[f] - halves[f] for f in range(6)], signal,
+        )
+        return [upper[f] - lower[f] for f in range(5)]
 
     def body(step):
         chunk = 2 * ROWS
@@ -322,7 +340,8 @@
             values = depth([state[step, f, at, :] for f in range(5)] + [own_p[at, :]], own_s[2, at, :])
             for f in range(5):
                 div[2, f, at, :] = values[f]
-        edges = gather_edges(lambda f, x: own_p[tile(x), :] if f == 0 else own_s[2, tile(x), :], 2)[0]
+        edge_p = edge_pack(lambda x: own_p[tile(x), :])
+        edge_s = edge_pack(lambda x: own_s[2, tile(x), :])
         kept_y = interior(1, emit_y)
         kept_x = interior(0, emit_x)
 
@@ -347,27 +366,15 @@
         for way in (1, 0):
             arrive(step, 2, way)
         arrive(step, 0, 0)
-        rim_packs = [jnp.where(early, got_z[step, 0, g], got_z[step, 1, g]) for g in range(3)]
-
-        def align(pack, f):
-            return pack[f // 2] if f % 2 == 0 else pltpu.roll(pack[f // 2], LANES // 2, 1)
-
-        rim = [align(rim_packs, f) for f in range(5)]
-        p, signals = state_eos(rim, shares_of(jnp.where(lower_half, align(rim_packs, 5), 1.0)))
-        outside = rim + [p, signals[2]]
-        inside = [align([pack_z[step, g] for g in range(3)], f) for f in range(5)]
-        inside += [edges, pltpu.roll(edges, LANES // 2, 1)]
-        window = [
-            jnp.where(
-                lower_half,
-                jnp.where(early, inside[f], outside[f]),
-                pltpu.roll(jnp.where(early, outside[f], inside[f]), LANES // 2, 1),
-            )
-            for f in range(7)
+        outside = [
+            jnp.where(lower_half, got_z[step, 1, f], got_z[step, 0, f]) for f in range(sent(step))
         ]
-        ends = [
-            jnp.where(early, v, pltpu.roll(v, LANES // 2, 1)) for v in depth(window[:6], window[6])
-        ]
+        if step == 0:
+            for k, value in enumerate(shares_of(outside.pop())):
+                shares_z[k] = value
+        p, signals = state_eos(outside, [shares_z[k] for k in range(3)])
+        window = [jnp.where(is_out, outside[f], pack_z[step, f]) for f in range(5)]
+        ends = rim_depth(window + [jnp.where(is_out, p, edge_p)], jnp.where(is_out, signals[2], edge_s))
         open_shares(0, got_x, shares_x)
         border(0, 0, got_x, shares_x, kept_x, emit_x)
 
@@ -375,7 +382,11 @@
         for x in (0, 1, ROWS - 2, ROWS - 1, *range(2, ROWS - 2)):
             at = tile(x)
             for f in range(5):
-                end = pltpu.roll(ends[f], (LANES - 4 - 8 * x) % LANES, 1)
+                end = jnp.where(
+                    at_low,
+                    pltpu.roll(ends[f], (half - 4 - 8 * x) % LANES, 1),
+                    pltpu.roll(ends[f], LANES - 4 - 8 * x, 1),
+                )
                 total = div[2, f, at, :] + jnp.where(at_edge, end, 0.0)
                 if not 2 <= x < ROWS - 2:
                     total = total + div[0, f, at, :]
@@ -430,15 +441,16 @@
             scratch_shapes=[
                 pltpu.VMEM((STEPS, 6, rows, nz), f32),
                 pltpu.VMEM((STEPS, 2, 6) + rim, f32),
-                pltpu.VMEM((STEPS, 3, ROWS, LANES), f32),
+                pltpu.VMEM((STEPS, 6, ROWS, LANES), f32),
                 pltpu.VMEM((STEPS, 2, 6) + rim, f32),
                 pltpu.VMEM((STEPS, 2, 6) + rim, f32),
-                pltpu.VMEM((STEPS, 2, 3, ROWS, LANES), f32),
+                pltpu.VMEM((STEPS, 2, 6, ROWS, LANES), f32),
                 pltpu.VMEM((rows, nz), jnp.int32),
                 pltpu.SMEM((STEPS,), jnp.int32),
                 pltpu.VMEM((3, rows, nz), f32),
                 pltpu.VMEM((2, 3) + rim, f32),
                 pltpu.VMEM((2, 3) + rim, f32),
+                pltpu.VMEM((3, ROWS, LANES), f32),
                 pltpu.VMEM((rows, nz), f32),
                 pltpu.VMEM((3, rows, nz), f32),
                 pltpu.VMEM((3, 5, rows, nz), f32),

time: 20.8 us -> 20.2 us (0.971)
  Pallas kernels: 20 us -> 19.5 us
    pallas_call x1, Pallas kernels: 19.3 us -> 18.8 us  [per_device(): pl.pallas_call(kernel, out_shape=pltpu.VMEM((5, rows, nz), f32), in_specs...]
where the time goes in v2:
time: 20.2 us; the launch traced here: 20.1 us
  Pallas kernels  19.5 us (97%)
  between operations  0.64 us (3%)
    pallas_call x1, Pallas kernels, per_device(): pl.pallas_call(kernel, out_shape=pltpu.VMEM((5, rows, nz), f32), in_specs...  18.8 us
    pallas_call x1, Pallas kernels, per_device(): pl.pallas_call(store, out_shape=tuple((jax.ShapeDtypeStruct((n, rows, nz)...  0.69 us

profile of v2, /device:TPU:0, one launch (start us, length us, event | category | flops | bytes accessed | tf_op | source)
XLA Modules:
  0.0 20.1 jit_solution(3266735551900650324)
XLA Ops:
  0.6 18.8 %hydro_steps.1.final = f32[5,64,128]{2,1,0:T(8,128)S(1)} custom-call(f32[1,64,128]{2,1,0:T(8,128)} %bitcast.8, f32[3,64,128]{2,1,0:T(8,128)} %bitcast.7, f32[1,64,128]{2,1,0:T(8,128)} %bitcast.9, s32[64,128]{1,0:T(8,128)} %bitcast.10, s32[3]{0:T(128)} %ticks_hbm.1), custom_call_target="tpu_custom_call" | custom-call | tf_op jit(solution)/shard_map/hydro_steps/pallas_call | solution.py:436
  19.4 0.7 %store_state.1 = (f32[1,64,128]{2,1,0:T(8,128)}, f32[3,64,128]{2,1,0:T(8,128)}, f32[1,64,128]{2,1,0:T(8,128)}) custom-call(f32[5,64,128]{2,1,0:T(8,128)S(1)} %hydro_steps.1.final), custom_call_target="tpu_custom_call" | custom-call | tf_op jit(solution)/shard_map/store_state/pallas_call | solution.py:470

commit v3 on v2

--- a/solution.py
+++ b/solution.py
@@ -160,17 +160,21 @@
     octet = lax.div(lane, 8)
     half = LANES // 2
     lower_half = lane < half
-    is_out = lax.div(lane, half) + lax.div(lax.rem(lane, 8), 4) == 1
-    at_low = lane < 2
-    at_edge = at_low | (lane >= LANES - 2)
-
-    def edge_pack(read):
-        total = None
-        for x in range(ROWS):
-            for start in (8 * x, half + 8 * x):
-                moved = pltpu.roll(read(x), start + 4, 1)
-                total = moved if total is None else jnp.where(octet == start // 8, moved, total)
+    spot = lax.rem(lane, 8)
+    is_out = lax.div(lane, half) + lax.div(spot, 4) == 1
+    inner = (spot >= 2) & (spot < 6)
+    at_edge = (lane < 2) | (lane >= LANES - 2)
+
+    def place(read, picked, starts, total=None):
+        for x in picked:
+            for start in starts:
+                moved = pltpu.roll(read(x), (start + 8 * x + 4) % LANES, 1)
+                total = moved if total is None else jnp.where(octet == start // 8 + x, moved, total)
         return total
+
+    def edge_pack(read, picked=range(ROWS)):
+        total = place(read, picked, (0,))
+        return jnp.where(lower_half, total, pltpu.roll(total, half, 1))
 
     def tile(x):
         return pl.ds(x * ROWS, ROWS)
@@ -196,8 +200,8 @@
         return pltpu.make_async_remote_copy(
             src_ref=src,
             dst_ref=into.at[fields],
-            send_sem=send_sem.at[step, a, way],
-            recv_sem=recv_sem.at[step, a, 1 - way],
+            send_sem=send_sem.at[a, way],
+            recv_sem=recv_sem.at[step % 2, a, 1 - way],
             device_id=peer(AXES[a], way),
             device_id_type=MESH,
         )
@@ -217,14 +221,11 @@
                         step, f, strided(k if way == 0 else ROWS - 2 + k), :
                     ]
 
-    def pack(step):
-        for f in range(sent(step)):
-            pack_z[step, f] = edge_pack(lambda x: state[step, f, tile(x), :])
-
     for load in loads:
         load.wait()
     state[0, 5] = mask_raw[...].astype(jnp.float32)
-    pack(0)
+    for f in range(6):
+        pack_z[0, f] = edge_pack(lambda x: state[0, f, tile(x), :])
     stage(0)
     pl.semaphore_wait(barrier, 6)
     for a in (2, 0, 1):
@@ -345,23 +346,39 @@
         kept_y = interior(1, emit_y)
         kept_x = interior(0, emit_x)
 
+        for a in (2, 0, 1):
+            for way in range(2):
+                rim_copy(step, a, way).wait_send()
         for way in (1, 0):
             arrive(step, 1, way)
         for way in (1, 0):
             open_shares(way, got_y, shares_y)
             border(1, way, got_y, shares_y, kept_y, emit_y)
         scale = ticks[step].astype(jnp.float32) * TIME_UNIT * 0.5
-        for x in range(ROWS):
-            at = tile(x)
-            for f in range(5):
-                part = div[1, f, at, :] + jnp.where(at_edge, 0.0, div[2, f, at, :])
-                if 2 <= x < ROWS - 2:
-                    part = part + div[0, f, at, :]
-                div[2, f, at, :] = part
+        last = step + 1 == STEPS
+        middle = range(2, ROWS - 2)
+
+        def settle(picked):
+            for x in picked:
+                at = tile(x)
+                for f in range(5):
+                    total = div[0, f, at, :] + div[1, f, at, :] + jnp.where(at_edge, 0.0, div[2, f, at, :])
+                    div[2, f, at, :] = state[step, f, at, :] - scale * total
+
+        def settled(f):
+            return lambda x: div[2, f, tile(x), :]
+
+        settle(middle)
+        if not last:
+            packs = [place(settled(f), middle, (0,)) for f in range(5)]
 
         arrive(step, 0, 1)
         open_shares(1, got_x, shares_x)
         border(0, 1, got_x, shares_x, kept_x, emit_x)
+        settle((ROWS - 2, ROWS - 1))
+        if not last:
+            packs = [place(settled(f), (ROWS - 2, ROWS - 1), (0,), packs[f]) for f in range(5)]
+            packs = [jnp.where(lower_half, v, pltpu.roll(v, half, 1)) for v in packs]
 
         for way in (1, 0):
             arrive(step, 2, way)
@@ -378,19 +395,19 @@
         open_shares(0, got_x, shares_x)
         border(0, 0, got_x, shares_x, kept_x, emit_x)
 
-        last = step + 1 == STEPS
-        for x in (0, 1, ROWS - 2, ROWS - 1, *range(2, ROWS - 2)):
+        settle((0, 1))
+        ends = [
+            jnp.where(inner, scale * jnp.where(is_out, pltpu.roll(v, half, 1), v), 0.0) for v in ends
+        ]
+        if not last:
+            for f in range(5):
+                pack_z[step + 1, f] = place(settled(f), (0, 1), (0, half), packs[f]) - ends[f]
+            send(step + 1, 2)
+        for x in (0, 1, ROWS - 2, ROWS - 1, *middle):
             at = tile(x)
             for f in range(5):
-                end = jnp.where(
-                    at_low,
-                    pltpu.roll(ends[f], (half - 4 - 8 * x) % LANES, 1),
-                    pltpu.roll(ends[f], LANES - 4 - 8 * x, 1),
-                )
-                total = div[2, f, at, :] + jnp.where(at_edge, end, 0.0)
-                if not 2 <= x < ROWS - 2:
-                    total = total + div[0, f, at, :]
-                value = state[step, f, at, :] - scale * total
+                end = pltpu.roll(ends[f], (LANES - 4 - 8 * x) % LANES, 1)
+                value = div[2, f, at, :] - jnp.where(at_edge, end, 0.0)
                 if last:
                     final[f, at, :] = value
                 else:
@@ -398,18 +415,11 @@
             if x == ROWS - 1 and not last:
                 send(step + 1, 0)
         if not last:
-            pack(step + 1)
-            send(step + 1, 2)
             stage(step + 1)
             send(step + 1, 1)
 
     for step in range(STEPS):
         body(step)
-
-    for way in range(2):
-        for a in range(3):
-            for step in range(STEPS):
-                rim_copy(step, a, way).wait_send()
 
 
 def store(final, density, momentum, energy, sem):
@@ -454,8 +464,8 @@
                 pltpu.VMEM((rows, nz), f32),
                 pltpu.VMEM((3, rows, nz), f32),
                 pltpu.VMEM((3, 5, rows, nz), f32),
-                pltpu.SemaphoreType.DMA((STEPS, 3, 2)),
-                pltpu.SemaphoreType.DMA((STEPS, 3, 2)),
+                pltpu.SemaphoreType.DMA((3, 2)),
+                pltpu.SemaphoreType.DMA((2, 3, 2)),
                 pltpu.SemaphoreType.DMA((5,)),
             ],
             compiler_params=pltpu.CompilerParams(collective_id=0, has_side_effects=True),

time: 20.2 us -> 20 us (0.990)
  Pallas kernels: 19.5 us -> 19.2 us
    pallas_call x1, Pallas kernels: 18.8 us -> 18.5 us  [per_device(): pl.pallas_call(kernel, out_shape=pltpu.VMEM((5, rows, nz), f32), in_specs...]
where the time goes in v3:
time: 20 us; the launch traced here: 19.8 us
  Pallas kernels  19.2 us (96%)
  between operations  0.64 us (3%)
    pallas_call x1, Pallas kernels, per_device(): pl.pallas_call(kernel, out_shape=pltpu.VMEM((5, rows, nz), f32), in_specs...  18.5 us
    pallas_call x1, Pallas kernels, per_device(): pl.pallas_call(store, out_shape=tuple((jax.ShapeDtypeStruct((n, rows, nz)...  0.69 us

profile of v3, /device:TPU:0, one launch (start us, length us, event | category | flops | bytes accessed | tf_op | source)
XLA Modules:
  0.0 19.8 jit_solution(1035992164797862998)
XLA Ops:
  0.6 18.5 %hydro_steps.1.final = f32[5,64,128]{2,1,0:T(8,128)S(1)} custom-call(f32[1,64,128]{2,1,0:T(8,128)} %bitcast.8, f32[3,64,128]{2,1,0:T(8,128)} %bitcast.7, f32[1,64,128]{2,1,0:T(8,128)} %bitcast.9, s32[64,128]{1,0:T(8,128)} %bitcast.10, s32[3]{0:T(128)} %ticks_hbm.1), custom_call_target="tpu_custom_call" | custom-call | tf_op jit(solution)/shard_map/hydro_steps/pallas_call | solution.py:446
  19.1 0.7 %store_state.1 = (f32[1,64,128]{2,1,0:T(8,128)}, f32[3,64,128]{2,1,0:T(8,128)}, f32[1,64,128]{2,1,0:T(8,128)}) custom-call(f32[5,64,128]{2,1,0:T(8,128)S(1)} %hydro_steps.1.final), custom_call_target="tpu_custom_call" | custom-call | tf_op jit(solution)/shard_map/store_state/pallas_call | solution.py:480
